TPU v7x, 512 devices: a whole 4x4x16 slice. The times are simulated.
512 devices in a mesh: dp: 32 (over z, core), seq: 16 (over y, x).
Axes of the slice: x: 4, y: 4, z: 16, core: 2. Of those that a mesh axis runs over, the one named last changes fastest.
Arguments:
- q_pre: bfloat16 [32, 2048, 16, 128], P('dp', 'seq'), may hold values from -6 to 6
- k_pre: bfloat16 [32, 2048, 8, 128], P('dp', 'seq'), may hold values from -6 to 6
- values: bfloat16 [32, 2048, 8, 128], P('dp', 'seq'), may hold values from -6 to 6
- grad_out: bfloat16 [32, 2048, 16, 128], P('dp', 'seq'), may hold values from -6 to 6
- segment_ids: int32 [32, 2048], P('dp', 'seq'), may hold values from 0 to 7, never falling along the last dimension, each value on 1 to 1024 neighbouring positions
- q_gain: float32 [128], replicated, may hold values from 0.1 to 1.9
- k_gain: float32 [128], replicated, may hold values from 0.1 to 1.9
Outputs:
- grad_q: bfloat16 [32, 2048, 16, 128], P('dp', 'seq')
- grad_k: bfloat16 [32, 2048, 8, 128], P('dp', 'seq')
- grad_v: bfloat16 [32, 2048, 8, 128], P('dp', 'seq')
- grad_q_gain: float32 [128], replicated
- grad_k_gain: float32 [128], replicated
Inputs may be any that keep to these rules, and one draw needn't show every extreme that they name: `segment_ids`: along a span the ids never fall, and each id from 0 to 7 names one run of consecutive tokens.
All inputs are finite; a program needn't handle non-finite values.
Results may differ from a plain program's by a relative error of at most 0.017.
Values may be sent and summed in bfloat16 or wider, within the bound.
A program may use at most 64 MiB of HBM per device.

v0:
```python
import jax
import jax.numpy as jnp
from jax import lax
from jax.sharding import PartitionSpec as P

PRESCALE = 168
DOCS = 8
norm_epsilon = 1e-06
rope_base = 1000000.0
rope_factor = 8.0


def document_positions(segments, docs):
    labels = jnp.arange(docs, dtype=jnp.int32)
    member = (segments[:, None] == labels[None, :]).astype(jnp.int32)
    counts = jnp.sum(member, axis=0)
    starts = jnp.cumsum(counts) - counts
    first = jnp.sum(member * starts[None, :], axis=1)
    return (jnp.arange(segments.shape[0], dtype=jnp.int32) - first, first)


def embed(rows, gain, positions):
    width = rows.shape[-1]
    half = width // 2
    scale = lax.rsqrt(jnp.mean(rows * rows, axis=-1, keepdims=True) + norm_epsilon)
    normed = rows * scale * gain
    freqs = rope_base ** (-(jnp.arange(half, dtype=jnp.float32) * 2.0 / width))
    angles = (positions.astype(jnp.float32) / rope_factor)[:, None] * freqs[None, :]
    cosine = jnp.cos(angles)[:, None, :]
    sine = jnp.sin(angles)[:, None, :]
    first_half = normed[..., :half]
    second_half = normed[..., half:]
    return jnp.concatenate(
        [first_half * cosine - second_half * sine, second_half * cosine + first_half * sine],
        axis=-1,
    )


def attend_blocks(queries, keys, vals, upstream, segments):
    total = queries.shape[0]
    group = queries.shape[1]
    width = queries.shape[2]
    block = min(512, total)
    count = total // block
    rows = block * group
    score_scale = float(PRESCALE) ** (-0.5)
    contract_last = (((1,), (1,)), ((), ()))
    contract_first = (((0,), (0,)), ((), ()))

    def query_block(query_index, carry):
        query_grads, key_grads, value_grads = carry
        start = query_index * block
        query_rows = lax.dynamic_slice_in_dim(queries, start, block, 0).reshape(rows, width)
        upstream_rows = lax.dynamic_slice_in_dim(upstream, start, block, 0).reshape(rows, width)
        query_segs = jnp.repeat(lax.dynamic_slice_in_dim(segments, start, block, 0), group)
        query_places = jnp.repeat(start + jnp.arange(block, dtype=jnp.int32), group)
        lower = 0

        def key_scores(key_index):
            key_start = key_index * block
            key_rows = lax.dynamic_slice_in_dim(keys, key_start, block, 0)
            value_rows = lax.dynamic_slice_in_dim(vals, key_start, block, 0)
            key_segs = lax.dynamic_slice_in_dim(segments, key_start, block, 0)
            key_places = key_start + jnp.arange(block, dtype=jnp.int32)
            scores = score_scale * lax.dot_general(
                query_rows, key_rows, contract_last, preferred_element_type=jnp.float32
            )
            visible = (query_segs[:, None] == key_segs[None, :]) & (
                query_places[:, None] >= key_places[None, :]
            )
            return (scores, visible, key_rows, value_rows, key_start)

        def forward_step(key_index, state):
            totals, numer = state
            scores, visible, key_rows, value_rows, key_start = key_scores(key_index)
            raw = jnp.where(visible, jnp.exp(scores), 0.0)
            numer = numer + jnp.dot(
                raw.astype(jnp.bfloat16), value_rows, preferred_element_type=jnp.float32
            )
            return (totals + jnp.sum(raw, axis=1), numer)

        totals, numer = lax.fori_loop(
            lower,
            query_index + 1,
            forward_step,
            (jnp.zeros((rows,), jnp.float32), jnp.zeros((rows, width), jnp.float32)),
        )
        outputs = numer / totals[:, None]
        delta = jnp.sum(upstream_rows.astype(jnp.float32) * outputs, axis=1)
        logsum = jnp.log(totals)

        def backward_step(key_index, state):
            query_part, key_acc, value_acc = state
            scores, visible, key_rows, value_rows, key_start = key_scores(key_index)
            probs = jnp.where(visible, jnp.exp(scores - logsum[:, None]), 0.0).astype(jnp.bfloat16)
            prob_grads = lax.dot_general(
                upstream_rows, value_rows, contract_last, preferred_element_type=jnp.float32
            )
            score_grads = (
                probs.astype(jnp.float32) * (prob_grads - delta[:, None]) * score_scale
            ).astype(jnp.bfloat16)
            query_part = query_part + jnp.dot(
                score_grads, key_rows, preferred_element_type=jnp.float32
            )
            key_part = lax.dot_general(
                score_grads, query_rows, contract_first, preferred_element_type=jnp.float32
            )
            value_part = lax.dot_general(
                probs, upstream_rows, contract_first, preferred_element_type=jnp.float32
            )
            key_acc = lax.dynamic_update_slice_in_dim(
                key_acc,
                lax.dynamic_slice_in_dim(key_acc, key_start, block, 0) + key_part,
                key_start,
                0,
            )
            value_acc = lax.dynamic_update_slice_in_dim(
                value_acc,
                lax.dynamic_slice_in_dim(value_acc, key_start, block, 0) + value_part,
                key_start,
                0,
            )
            return (query_part, key_acc, value_acc)

        query_part, key_grads, value_grads = lax.fori_loop(
            lower,
            query_index + 1,
            backward_step,
            (jnp.zeros((rows, width), jnp.float32), key_grads, value_grads),
        )
        query_grads = lax.dynamic_update_slice_in_dim(query_grads, query_part, start * group, 0)
        return (query_grads, key_grads, value_grads)

    initial = (
        jnp.zeros((total * group, width), jnp.float32),
        jnp.zeros((total, width), jnp.float32),
        jnp.zeros((total, width), jnp.float32),
    )
    query_grads, key_grads, value_grads = lax.fori_loop(0, count, query_block, initial)
    return (query_grads.reshape(total, group, width), key_grads, value_grads)


def body(q_pre, k_pre, values, grad_out, segment_ids, q_gain, k_gain):
    segments = lax.all_gather(segment_ids, "seq", axis=1, tiled=True)[0]
    positions, first = document_positions(segments, DOCS)
    local = q_pre.shape[1]
    heads = q_pre.shape[2]
    kv_heads = k_pre.shape[2]
    width = q_pre.shape[3]
    group = heads // kv_heads

    def embed_rows(rows, gain):
        return embed(rows, gain, positions)

    key_copies = jnp.repeat(k_pre[0], group, axis=1)
    value_copies = jnp.repeat(values[0], group, axis=1)
    query_here, upstream_here, key_here, value_here = (
        lax.all_to_all(q_pre[0], "seq", split_axis=1, concat_axis=0, tiled=True),
        lax.all_to_all(grad_out[0], "seq", split_axis=1, concat_axis=0, tiled=True),
        lax.all_to_all(key_copies, "seq", split_axis=1, concat_axis=0, tiled=True),
        lax.all_to_all(value_copies, "seq", split_axis=1, concat_axis=0, tiled=True),
    )
    query_rot, query_back = jax.vjp(embed_rows, query_here.astype(jnp.float32), q_gain)
    key_rot, key_back = jax.vjp(embed_rows, key_here.astype(jnp.float32), k_gain)
    query_hat = query_rot.astype(jnp.bfloat16)
    key_hat = key_rot.astype(jnp.bfloat16)
    query_list, key_list, value_list = ([], [], [])
    query_part, key_part, value_part = attend_blocks(
        query_hat, key_hat[:, 0], value_here[:, 0], upstream_here, segments
    )
    query_list.append(query_part)
    key_list.append(key_part)
    value_list.append(value_part)
    query_input, query_gain_part = query_back(query_list[0])
    key_input, key_gain_part = key_back(jnp.stack(key_list, axis=1))
    value_input = jnp.stack(value_list, axis=1)
    query_return, key_return, value_return = (
        lax.all_to_all(
            query_input.astype(jnp.bfloat16), "seq", split_axis=0, concat_axis=1, tiled=True
        ).astype(query_input.dtype),
        lax.all_to_all(
            key_input.astype(jnp.bfloat16), "seq", split_axis=0, concat_axis=1, tiled=True
        ).astype(key_input.dtype),
        lax.all_to_all(
            value_input.astype(jnp.bfloat16), "seq", split_axis=0, concat_axis=1, tiled=True
        ).astype(value_input.dtype),
    )
    grad_q = query_return.astype(jnp.bfloat16)
    grad_k = jnp.sum(key_return.reshape(local, kv_heads, group, width), axis=2).astype(jnp.bfloat16)
    grad_v = jnp.sum(value_return.reshape(local, kv_heads, group, width), axis=2).astype(
        jnp.bfloat16
    )
    gain_totals = lax.psum((query_gain_part, key_gain_part), ("dp", "seq"))
    return (grad_q[None], grad_k[None], grad_v[None], gain_totals[0], gain_totals[1])


def solution(mesh):
    return jax.shard_map(
        body,
        mesh=mesh,
        in_specs=(
            P("dp", "seq", None, None),
            P("dp", "seq", None, None),
            P("dp", "seq", None, None),
            P("dp", "seq", None, None),
            P("dp", "seq"),
            P(),
            P(),
        ),
        out_specs=(
            P("dp", "seq", None, None),
            P("dp", "seq", None, None),
            P("dp", "seq", None, None),
            P(),
            P(),
        ),
        check_vma=False,
    )
```

profile of v0, /device:TPU:1, one launch (start us, length us, event | category | flops | bytes accessed | tf_op | source)
XLA Modules:
  0.0 308.5 jit_solution(509402824562934716)
XLA Ops:
  0.6 2.0 copy.172
  2.6 7.7 %all-to-all-start = ((bf16[128,16,128]{2,0,1:T(8,128)(2,1)}), bf16[128,16,128]{2,0,1:T(8,128)(2,1)S(1)}, u32[]{:S(2)}, u32[]{:S(2)}) async-start(bf16[128,16,128]{2,0,1:T(8,128)(2,1)} %bitcast.130), calls=%async_computation | async-start | bytes 1048576 | tf_op jit(solution)/shard_map/all_to_all | solution.py:158
  10.4 17.6 %all_gather.3 = s32[1,2048]{1,0:T(1,128)S(1)} all-gather(s32[1,128]{1,0:T(1,128)S(1)} %copy-done.13), channel_id=1, replica_groups=mesh['dp'=32,'seq'=16] {'seq'}, dimensions={1}, use_global_device_ids=true | all-gather | bytes 8704 | tf_op jit(solution)/shard_map/all_gather | solution.py:144
  31.3 4.0 %all-to-all-start.1 = ((bf16[128,16,128]{0,2,1:T(8,128)(2,1)}), bf16[128,16,128]{0,2,1:T(8,128)(2,1)S(1)}, u32[]{:S(2)}, u32[]{:S(2)}) async-start(bf16[128,16,128]{0,2,1:T(8,128)(2,1)} %bitcast.12), calls=%async_computation.1 | async-start | bytes 1048576 | tf_op jit(solution)/shard_map/all_to_all | solution.py:160
  37.4 6.9 %all-to-all-done.1 = bf16[128,16,128]{0,2,1:T(8,128)(2,1)S(1)} async-done(((bf16[128,16,128]{0,2,1:T(8,128)(2,1)}), bf16[128,16,128]{0,2,1:T(8,128)(2,1)S(1)}, u32[]{:S(2)}, u32[]{:S(2)}) %all-to-all-start.1) | async-done | bytes 524320 | tf_op jit(solution)/shard_map/all_to_all | solution.py:160
  45.3 3.6 %all-to-all-start.2 = ((bf16[128,16,128]{2,0,1:T(8,128)(2,1)}), bf16[128,16,128]{2,0,1:T(8,128)(2,1)S(1)}, u32[]{:S(2)}, u32[]{:S(2)}) async-start(bf16[128,16,128]{2,0,1:T(8,128)(2,1)} %bitcast.20), calls=%async_computation.2 | async-start | bytes 1048576 | tf_op jit(solution)/shard_map/all_to_all | solution.py:161
  50.8 7.0 %all-to-all-done.2 = bf16[128,16,128]{2,0,1:T(8,128)(2,1)S(1)} async-done(((bf16[128,16,128]{2,0,1:T(8,128)(2,1)}), bf16[128,16,128]{2,0,1:T(8,128)(2,1)S(1)}, u32[]{:S(2)}, u32[]{:S(2)}) %all-to-all-start.2) | async-done | bytes 524320 | tf_op jit(solution)/shard_map/all_to_all | solution.py:161
  57.8 4.2 %all-to-all-start.3 = ((bf16[128,16,128]{2,0,1:T(8,128)(2,1)}), bf16[128,16,128]{2,0,1:T(8,128)(2,1)}, u32[]{:S(2)}, u32[]{:S(2)}) async-start(bf16[128,16,128]{2,0,1:T(8,128)(2,1)} %bitcast.129), calls=%async_computation.3 | async-start | bytes 1048576 | tf_op jit(solution)/shard_map/all_to_all | solution.py:159
  62.1 3.1 fusion.63
  66.2 4.8 %all-to-all-done.3 = bf16[128,16,128]{2,0,1:T(8,128)(2,1)} async-done(((bf16[128,16,128]{2,0,1:T(8,128)(2,1)}), bf16[128,16,128]{2,0,1:T(8,128)(2,1)}, u32[]{:S(2)}, u32[]{:S(2)}) %all-to-all-start.3) | async-done | bytes 524320 | tf_op jit(solution)/shard_map/all_to_all | solution.py:159
  72.3 69.1 %while.79 = (s32[]{:T(128)}, f32[2048,128]{0,1:T(8,128)}, f32[2048,128]{1,0:T(8,128)S(1)}, f32[2048,128]{1,0:T(8,128)S(1)}, bf16[2048,1,128]{0,2,1:T(8,128)(2,1)...) while((s32[]{:T(128)}, f32[2048,128]{0,1:T(8,128)}, ...), condition=%wide.region_12.13_spmd, body=%wide.region_5.12_spmd.sunk | while | flops 475268608 | bytes 14478353 | solution.py:139
  73.2 1.9 while.80
  73.3 1.4 fusion.101
  76.3 3.7 %while.81 = (s32[]{:T(128)}, f32[512,128]{1,0:T(8,128)S(1)}, f32[2048,128]{1,0:T(8,128)S(1)}, f32[2048,128]{1,0:T(8,128)S(1)}, s32[]{:T(128)}, /*index=5*/s32[51...) while((s32[]{:T(128)}, f32[512,128]{1,0:T(8,128)S(1)}, ...), condition=%wide.region_11.11_spmd.clone, body=%wide.region_10.10_spmd.clone.sunk | while | flops 338887680 | bytes 5656819 | solution.py:125
  82.1 3.7 %while.80 = (s32[]{:T(128)}, f32[512]{0:T(512)S(1)}, f32[512,128]{1,0:T(8,128)S(1)}, s32[]{:T(128)}, s32[512]{0:T(512)S(1)}, /*index=5*/s32[2048]{0:T(1024)S(1)}...) while((s32[]{:T(128)}, f32[512]{0:T(512)S(1)}, ...), condition=%wide.region_8.8_spmd.clone, body=%wide.region_6.7_spmd.clone.sunk | while | flops 136119296 | bytes 1990855 | solution.py:82
  82.2 1.4 fusion.101
  84.1 1.4 fusion.101
  87.0 7.4 %while.81 = (s32[]{:T(128)}, f32[512,128]{1,0:T(8,128)S(1)}, f32[2048,128]{1,0:T(8,128)S(1)}, f32[2048,128]{1,0:T(8,128)S(1)}, s32[]{:T(128)}, /*index=5*/s32[51...) while((s32[]{:T(128)}, f32[512,128]{1,0:T(8,128)S(1)}, ...), condition=%wide.region_11.11_spmd.clone, body=%wide.region_10.10_spmd.clone.sunk | while | flops 338887680 | bytes 5656819 | solution.py:125
  96.6 5.6 %while.80 = (s32[]{:T(128)}, f32[512]{0:T(512)S(1)}, f32[512,128]{1,0:T(8,128)S(1)}, s32[]{:T(128)}, s32[512]{0:T(512)S(1)}, /*index=5*/s32[2048]{0:T(1024)S(1)}...) while((s32[]{:T(128)}, f32[512]{0:T(512)S(1)}, ...), condition=%wide.region_8.8_spmd.clone, body=%wide.region_6.7_spmd.clone.sunk | while | flops 136119296 | bytes 1990855 | solution.py:82
  98.6 1.4 fusion.101
  103.4 11.1 %while.81 = (s32[]{:T(128)}, f32[512,128]{1,0:T(8,128)S(1)}, f32[2048,128]{1,0:T(8,128)S(1)}, f32[2048,128]{1,0:T(8,128)S(1)}, s32[]{:T(128)}, /*index=5*/s32[51...) while((s32[]{:T(128)}, f32[512,128]{1,0:T(8,128)S(1)}, ...), condition=%wide.region_11.11_spmd.clone, body=%wide.region_10.10_spmd.clone.sunk | while | flops 338887680 | bytes 5656819 | solution.py:125
  116.6 7.5 %while.80 = (s32[]{:T(128)}, f32[512]{0:T(512)S(1)}, f32[512,128]{1,0:T(8,128)S(1)}, s32[]{:T(128)}, s32[512]{0:T(512)S(1)}, /*index=5*/s32[2048]{0:T(1024)S(1)}...) while((s32[]{:T(128)}, f32[512]{0:T(512)S(1)}, ...), condition=%wide.region_8.8_spmd.clone, body=%wide.region_6.7_spmd.clone.sunk | while | flops 136119296 | bytes 1990855 | solution.py:82
  116.7 1.4 fusion.101
  118.6 1.4 fusion.101
  125.3 14.8 %while.81 = (s32[]{:T(128)}, f32[512,128]{1,0:T(8,128)S(1)}, f32[2048,128]{1,0:T(8,128)S(1)}, f32[2048,128]{1,0:T(8,128)S(1)}, s32[]{:T(128)}, /*index=5*/s32[51...) while((s32[]{:T(128)}, f32[512,128]{1,0:T(8,128)S(1)}, ...), condition=%wide.region_11.11_spmd.clone, body=%wide.region_10.10_spmd.clone.sunk | while | flops 338887680 | bytes 5656819 | solution.py:125
  142.7 4.1 %fusion.60 = (f32[2048,1,64]{0,2,1:T(8,128)S(1)}, f32[2048,1,64]{0,2,1:T(8,128)S(1)}, f32[2048,1,64]{0,2,1:T(8,128)S(1)}, f32[2048,1,64]{0,2,1:T(8,128)S(1)}) fusion(f32[2048,1,128]{0,2,1:T(8,128)} %bitcast.158, f32[64]{0:T(128)S(1)} %negate_power_fusion, f32[2048]{0:T(1024)S(1)} %convert_multiply_fusion.1, f32[2048,1,128]{0,2,1:T(8,128)} %bitcast.157), kind=kLoop, calls=%fused_computation.89 | loop fusion | flops 1966080 | bytes 4202752 | tf_op jit(solution)/shard_map/transpose(jvp())/add_any | solution.py:34
  151.6 3.6 %all-to-all-start.4 = ((bf16[16,2,8192]{2,1,0:T(2,128)(2,1)}), bf16[16,2,8192]{2,1,0:T(2,128)(2,1)S(1)}, u32[]{:S(2)}, u32[]{:S(2)}) async-start(bf16[16,2,8192]{2,1,0:T(2,128)(2,1)} %reshape.576), calls=%async_computation.4 | async-start | bytes 1048576 | tf_op jit(solution)/shard_map/all_to_all | solution.py:178
  157.4 6.8 %all-to-all-done.4 = bf16[16,2,8192]{2,1,0:T(2,128)(2,1)S(1)} async-done(((bf16[16,2,8192]{2,1,0:T(2,128)(2,1)}), bf16[16,2,8192]{2,1,0:T(2,128)(2,1)S(1)}, u32[]{:S(2)}, u32[]{:S(2)}) %all-to-all-start.4) | async-done | bytes 524320 | tf_op jit(solution)/shard_map/all_to_all | solution.py:178
  164.1 3.6 %all-to-all-start.5 = ((bf16[16,2,8192]{2,1,0:T(2,128)(2,1)}), bf16[16,2,8192]{2,1,0:T(2,128)(2,1)S(1)}, u32[]{:S(2)}, u32[]{:S(2)}) async-start(bf16[16,2,8192]{2,1,0:T(2,128)(2,1)} %reshape.578), calls=%async_computation.5 | async-start | bytes 1048576 | tf_op jit(solution)/shard_map/all_to_all | solution.py:181
  169.7 9.0 %all-to-all-done.5 = bf16[16,2,8192]{2,1,0:T(2,128)(2,1)S(1)} async-done(((bf16[16,2,8192]{2,1,0:T(2,128)(2,1)}), bf16[16,2,8192]{2,1,0:T(2,128)(2,1)S(1)}, u32[]{:S(2)}, u32[]{:S(2)}) %all-to-all-start.5) | async-done | bytes 524320 | tf_op jit(solution)/shard_map/all_to_all | solution.py:181
  178.7 3.6 %all-to-all-start.6 = ((bf16[16,2,8192]{2,1,0:T(2,128)(2,1)}), bf16[16,2,8192]{2,1,0:T(2,128)(2,1)S(1)}, u32[]{:S(2)}, u32[]{:S(2)}) async-start(bf16[16,2,8192]{2,1,0:T(2,128)(2,1)} %reshape.580), calls=%async_computation.6 | async-start | bytes 1048576 | tf_op jit(solution)/shard_map/all_to_all | solution.py:184
  182.3 121.2 %all-reduce.4 = (f32[128]{0:T(128)}, f32[128]{0:T(128)}) all-reduce(f32[128]{0:T(128)S(1)} %get-tuple-element.430, f32[128]{0:T(128)S(1)} %get-tuple-element.428), channel_id=1, replica_groups=mesh['dp'=32,'seq'=16] {'dp','seq'}, use_global_device_ids=true, to_apply=%region_18.19 | all-reduce | flops 256 | bytes 2048 | tf_op jit(solution)/shard_map/psum | solution.py:193
  (248 shorter events, 85.4 us)
Async XLA Ops:
  2.6 7.7 %copy-start.13 = (s32[1,128]{1,0:T(1,128)S(1)}, s32[1,128]{1,0:T(1,128)}, u32[]{:S(2)}) copy-start(s32[1,128]{1,0:T(1,128)} %param.17) | copy-start | bytes 1540
  2.6 25.7 %copy-start.9 = (bf16[1,128,8,128]{3,2,1,0:T(8,128)(2,1)S(1)}, bf16[1,128,8,128]{3,2,1,0:T(8,128)(2,1)}, u32[]{:S(2)}) copy-start(bf16[1,128,8,128]{3,2,1,0:T(8,128)(2,1)} %param.14) | copy-start | bytes 786436
  2.6 27.8 %all-to-all-start = ((bf16[128,16,128]{2,0,1:T(8,128)(2,1)}), bf16[128,16,128]{2,0,1:T(8,128)(2,1)S(1)}, u32[]{:S(2)}, u32[]{:S(2)}) async-start(bf16[128,16,128]{2,0,1:T(8,128)(2,1)} %bitcast.130), calls=%async_computation | async-start | bytes 1048576 | tf_op jit(solution)/shard_map/all_to_all | solution.py:158
  10.3 18.2 %copy-start.10 = (bf16[1,128,8,128]{3,2,1,0:T(8,128)(2,1)S(1)}, bf16[1,128,8,128]{3,2,1,0:T(8,128)(2,1)}, u32[]{:S(2)}) copy-start(bf16[1,128,8,128]{3,2,1,0:T(8,128)(2,1)} %param.15) | copy-start | bytes 786436
  28.3 1.0 copy-start.8
  31.3 13.0 %all-to-all-start.1 = ((bf16[128,16,128]{0,2,1:T(8,128)(2,1)}), bf16[128,16,128]{0,2,1:T(8,128)(2,1)S(1)}, u32[]{:S(2)}, u32[]{:S(2)}) async-start(bf16[128,16,128]{0,2,1:T(8,128)(2,1)} %bitcast.12), calls=%async_computation.1 | async-start | bytes 1048576 | tf_op jit(solution)/shard_map/all_to_all | solution.py:160
  35.8 0.7 copy-start.12
  36.5 1.0 copy-start
  44.3 4.7 %copy-start.2 = (bf16[128,16,128]{0,2,1:T(8,128)(2,1)}, bf16[128,16,128]{0,2,1:T(8,128)(2,1)S(1)}, u32[]{:S(2)}) copy-start(bf16[128,16,128]{0,2,1:T(8,128)(2,1)S(1)} %all-to-all-done.1) | copy-start | bytes 1572868
  45.3 12.5 %all-to-all-start.2 = ((bf16[128,16,128]{2,0,1:T(8,128)(2,1)}), bf16[128,16,128]{2,0,1:T(8,128)(2,1)S(1)}, u32[]{:S(2)}, u32[]{:S(2)}) async-start(bf16[128,16,128]{2,0,1:T(8,128)(2,1)} %bitcast.20), calls=%async_computation.2 | async-start | bytes 1048576 | tf_op jit(solution)/shard_map/all_to_all | solution.py:161
  49.0 0.7 copy-start.11
  50.8 11.2 %copy-start.4 = (f32[2048,1,128]{0,2,1:T(8,128)S(1)}, f32[2048,1,128]{0,2,1:T(8,128)}, u32[]{:S(2)}) copy-start(f32[2048,1,128]{0,2,1:T(8,128)} %fusion.33) | copy-start | bytes 3145732
  57.8 13.2 %all-to-all-start.3 = ((bf16[128,16,128]{2,0,1:T(8,128)(2,1)}), bf16[128,16,128]{2,0,1:T(8,128)(2,1)}, u32[]{:S(2)}, u32[]{:S(2)}) async-start(bf16[128,16,128]{2,0,1:T(8,128)(2,1)} %bitcast.129), calls=%async_computation.3 | async-start | bytes 1048576 | tf_op jit(solution)/shard_map/all_to_all | solution.py:159
  65.2 1.0 copy-start.7
  72.4 0.8 copy-start.5
  80.1 1.1 copy-start.6
  81.3 0.8 copy-start.5
  94.6 1.1 copy-start.6
  95.7 0.8 copy-start.5
  114.6 1.1 copy-start.6
  115.8 0.8 copy-start.5
  140.3 1.1 copy-start.6
  142.7 4.1 %copy-start.3 = (bf16[128,16,128]{0,2,1:T(8,128)(2,1)S(1)}, bf16[128,16,128]{0,2,1:T(8,128)(2,1)}, u32[]{:S(2)}) copy-start(bf16[128,16,128]{0,2,1:T(8,128)(2,1)} %copy-done.2) | copy-start | bytes 1572868
  146.8 1.2 copy-start.1
  151.6 12.5 %all-to-all-start.4 = ((bf16[16,2,8192]{2,1,0:T(2,128)(2,1)}), bf16[16,2,8192]{2,1,0:T(2,128)(2,1)S(1)}, u32[]{:S(2)}, u32[]{:S(2)}) async-start(bf16[16,2,8192]{2,1,0:T(2,128)(2,1)} %reshape.576), calls=%async_computation.4 | async-start | bytes 1048576 | tf_op jit(solution)/shard_map/all_to_all | solution.py:178
  164.1 14.6 %all-to-all-start.5 = ((bf16[16,2,8192]{2,1,0:T(2,128)(2,1)}), bf16[16,2,8192]{2,1,0:T(2,128)(2,1)S(1)}, u32[]{:S(2)}, u32[]{:S(2)}) async-start(bf16[16,2,8192]{2,1,0:T(2,128)(2,1)} %reshape.578), calls=%async_computation.5 | async-start | bytes 1048576 | tf_op jit(solution)/shard_map/all_to_all | solution.py:181
  178.7 128.1 %all-to-all-start.6 = ((bf16[16,2,8192]{2,1,0:T(2,128)(2,1)}), bf16[16,2,8192]{2,1,0:T(2,128)(2,1)S(1)}, u32[]{:S(2)}, u32[]{:S(2)}) async-start(bf16[16,2,8192]{2,1,0:T(2,128)(2,1)} %reshape.580), calls=%async_computation.6 | async-start | bytes 1048576 | tf_op jit(solution)/shard_map/all_to_all | solution.py:184
where the time goes:
time: 310 us; the launch traced here: 308 us
  blocking collectives  139 us (45%)
  matrix products  53.1 us (17%)
  waiting for transfers between devices  34.4 us (11%)
  local copies, waits for them, and re-layouts  30.6 us (10%)
  starting transfers between devices  30.2 us (10%)
  other arithmetic  19 us (6%)
    psum x1, blocking collectives, body(): gain_totals = lax.psum((query_gain_part, key_gain_part), ('dp', 'seq'))  121 us
    dot_general x20, matrix products, key_scores(): lax.dot_general(query_rows, key_rows, contract_last, preferred_element_ty...  27.3 us
    all_gather x1, blocking collectives, body(): segments = lax.all_gather(segment_ids, 'seq', axis=1, tiled=True)[0]  17.6 us
    unnamed x40, local copies, waits for them, and re-layouts  14.1 us
    dot_general x10, matrix products, backward_step(): jnp.dot(score_grads, key_rows, preferred_element_type=jnp.float32)  12.8 us
    all_to_all x1, waiting for transfers between devices, body(): lax.all_to_all(key_input.astype(jnp.bfloat16), 'seq', split_axis=0, conca...  8.96 us
    all_to_all x1, starting transfers between devices, body(): lax.all_to_all(q_pre[0], 'seq', split_axis=1, concat_axis=0, tiled=True)  7.72 us
    all_to_all x1, waiting for transfers between devices, body(): lax.all_to_all(value_copies, 'seq', split_axis=1, concat_axis=0, tiled=True)  6.98 us
  transfers between devices with their start and end apart: 7, of which 5 were waited for; matrix products, arithmetic and copies ran while one was open for 5% of the time, Pallas kernels for 0%

commit v1 on v0

--- a/solution.py
+++ b/solution.py
@@ -141,7 +141,15 @@
 
 
 def body(q_pre, k_pre, values, grad_out, segment_ids, q_gain, k_gain):
-    segments = lax.all_gather(segment_ids, "seq", axis=1, tiled=True)[0]
+    segments = jnp.concatenate(
+        lax.all_to_all(
+            jnp.stack([segment_ids for _ in range(lax.axis_size("seq"))]),
+            axis_name="seq",
+            split_axis=0,
+            concat_axis=0,
+        ),
+        axis=1,
+    )[0]
     positions, first = document_positions(segments, DOCS)
     local = q_pre.shape[1]
     heads = q_pre.shape[2]

time: 310 us -> 305 us (0.984)
  blocking collectives: 139 us -> 117 us
  waiting for transfers between devices: 34.4 us -> 41 us
  starting transfers between devices: 30.2 us -> 34.1 us
  other arithmetic: 19 us -> 22.9 us
    all_gather x1 -> x0, blocking collectives: 17.6 us -> none  [body(): segments = lax.all_gather(segment_ids, 'seq', axis=1, tiled=True)[0]]
    all_to_all x1, waiting for transfers between devices: 0.01 us -> 8.56 us  [body(): lax.all_to_all(q_pre[0], 'seq', split_axis=1, concat_axis=0, tiled=True)]
    all_to_all x0 -> x1, starting transfers between devices: none -> 7.58 us  [body(): lax.all_to_all(jnp.stack([segment_ids for _ in range(lax.axis_size('seq')...]
    psum x1, blocking collectives: 121 us -> 117 us  [body(): gain_totals = lax.psum((query_gain_part, key_gain_part), ('dp', 'seq'))]
    all_to_all x1, starting transfers between devices: 7.72 us -> 4.43 us  [body(): lax.all_to_all(q_pre[0], 'seq', split_axis=1, concat_axis=0, tiled=True)]
    unnamed x40 -> x44, local copies, waits for them, and re-layouts: 14.1 us -> 12.9 us
  transfers between devices with their start and end apart: 7 -> 8, of which waited for: 5 -> 7; matrix products, arithmetic and copies ran while one was open for 5% -> 7% of each run, Pallas kernels for 0% -> 0%
where the time goes in v1:
time: 305 us; the launch traced here: 302 us
  blocking collectives  117 us (38%)
  matrix products  53.1 us (17%)
  waiting for transfers between devices  41 us (13%)
  starting transfers between devices  34.1 us (11%)
  local copies, waits for them, and re-layouts  32.1 us (11%)
  other arithmetic  22.9 us (8%)
    psum x1, blocking collectives, body(): gain_totals = lax.psum((query_gain_part, key_gain_part), ('dp', 'seq'))  117 us
    dot_general x20, matrix products, key_scores(): lax.dot_general(query_rows, key_rows, contract_last, preferred_element_ty...  27.3 us
    unnamed x44, local copies, waits for them, and re-layouts  12.9 us
    dot_general x10, matrix products, backward_step(): jnp.dot(score_grads, key_rows, preferred_element_type=jnp.float32)  12.8 us
    all_to_all x1, waiting for transfers between devices, body(): lax.all_to_all(q_pre[0], 'seq', split_axis=1, concat_axis=0, tiled=True)  8.56 us
    all_to_all x1, starting transfers between devices, body(): lax.all_to_all(jnp.stack([segment_ids for _ in range(lax.axis_size('seq')...  7.58 us
    all_to_all x1, waiting for transfers between devices, body(): lax.all_to_all(value_copies, 'seq', split_axis=1, concat_axis=0, tiled=True)  7.03 us
    all_to_all x1, waiting for transfers between devices, body(): lax.all_to_all(key_input.astype(jnp.bfloat16), 'seq', split_axis=0, conca...  6.93 us
  transfers between devices with their start and end apart: 8, of which 7 were waited for; matrix products, arithmetic and copies ran while one was open for 7% of the time, Pallas kernels for 0%

profile of v1, /device:TPU:1, one launch (start us, length us, event | category | flops | bytes accessed | tf_op | source)
XLA Modules:
  0.0 302.5 jit_solution(2113326433874825028)
XLA Ops:
  1.9 7.6 %all-to-all-start.1 = ((s32[16,1,128]{2,1,0:T(1,128)}), s32[16,1,128]{2,1,0:T(1,128)S(1)}, u32[]{:S(2)}, u32[]{:S(2)}) async-start(s32[16,1,128]{2,1,0:T(1,128)} %stack.4), calls=%async_computation.1 | async-start | bytes 16384 | tf_op jit(solution)/shard_map/all_to_all | solution.py:145
  13.6 2.2 all-to-all-done.1
  15.8 4.4 %all-to-all-start = ((bf16[128,16,128]{2,0,1:T(8,128)(2,1)}), bf16[128,16,128]{2,0,1:T(8,128)(2,1)S(1)}, u32[]{:S(2)}, u32[]{:S(2)}) async-start(bf16[128,16,128]{2,0,1:T(8,128)(2,1)} %bitcast.131), calls=%async_computation | async-start | bytes 1048576 | tf_op jit(solution)/shard_map/all_to_all | solution.py:166
  20.7 8.6 %all-to-all-done = bf16[128,16,128]{2,0,1:T(8,128)(2,1)S(1)} async-done(((bf16[128,16,128]{2,0,1:T(8,128)(2,1)}), bf16[128,16,128]{2,0,1:T(8,128)(2,1)S(1)}, u32[]{:S(2)}, u32[]{:S(2)}) %all-to-all-start) | async-done | bytes 524320 | tf_op jit(solution)/shard_map/all_to_all | solution.py:166
  30.1 3.6 %all-to-all-start.2 = ((bf16[128,16,128]{0,2,1:T(8,128)(2,1)}), bf16[128,16,128]{0,2,1:T(8,128)(2,1)S(1)}, u32[]{:S(2)}, u32[]{:S(2)}) async-start(bf16[128,16,128]{0,2,1:T(8,128)(2,1)} %bitcast.13), calls=%async_computation.2 | async-start | bytes 1048576 | tf_op jit(solution)/shard_map/all_to_all | solution.py:168
  35.2 1.6 copy.145
  38.1 4.7 %all-to-all-done.2 = bf16[128,16,128]{0,2,1:T(8,128)(2,1)S(1)} async-done(((bf16[128,16,128]{0,2,1:T(8,128)(2,1)}), bf16[128,16,128]{0,2,1:T(8,128)(2,1)S(1)}, u32[]{:S(2)}, u32[]{:S(2)}) %all-to-all-start.2) | async-done | bytes 524320 | tf_op jit(solution)/shard_map/all_to_all | solution.py:168
  43.7 3.6 %all-to-all-start.3 = ((bf16[128,16,128]{2,0,1:T(8,128)(2,1)}), bf16[128,16,128]{2,0,1:T(8,128)(2,1)S(1)}, u32[]{:S(2)}, u32[]{:S(2)}) async-start(bf16[128,16,128]{2,0,1:T(8,128)(2,1)} %bitcast.21), calls=%async_computation.3 | async-start | bytes 1048576 | tf_op jit(solution)/shard_map/all_to_all | solution.py:169
  49.2 7.0 %all-to-all-done.3 = bf16[128,16,128]{2,0,1:T(8,128)(2,1)S(1)} async-done(((bf16[128,16,128]{2,0,1:T(8,128)(2,1)}), bf16[128,16,128]{2,0,1:T(8,128)(2,1)S(1)}, u32[]{:S(2)}, u32[]{:S(2)}) %all-to-all-start.3) | async-done | bytes 524320 | tf_op jit(solution)/shard_map/all_to_all | solution.py:169
  56.3 4.2 %all-to-all-start.4 = ((bf16[128,16,128]{2,0,1:T(8,128)(2,1)}), bf16[128,16,128]{2,0,1:T(8,128)(2,1)}, u32[]{:S(2)}, u32[]{:S(2)}) async-start(bf16[128,16,128]{2,0,1:T(8,128)(2,1)} %bitcast.130), calls=%async_computation.4 | async-start | bytes 1048576 | tf_op jit(solution)/shard_map/all_to_all | solution.py:167
  60.5 3.1 %fusion.63 = (bf16[2048,64]{0,1:T(8,128)(2,1)S(1)}, bf16[2048,64]{0,1:T(8,128)(2,1)S(1)}, bf16[2048,1,64]{0,2,1:T(8,128)(2,1)}, bf16[2048,1,64]{0,2,1:T(8,128)(2,1)}) fusion(f32[2048,1,128]{0,2,1:T(8,128)S(1)} %copy-done.5, f32[64]{0:T(128)S(1)} %negate_power_fusion, f32[2048]{0:T(1024)S(1)} %convert_multiply_fusion.1, f32[2048,1,128]{0,2,1:T(8,128)S(1)} %copy-done.4), kind=kLoop, calls=%fused_computation.97 | loop fusion | flops 2228224 | bytes 3154176 | tf_op jit(solution)/shard_map/jvp()/concatenate | solution.py:33
  64.8 4.8 %all-to-all-done.4 = bf16[128,16,128]{2,0,1:T(8,128)(2,1)} async-done(((bf16[128,16,128]{2,0,1:T(8,128)(2,1)}), bf16[128,16,128]{2,0,1:T(8,128)(2,1)}, u32[]{:S(2)}, u32[]{:S(2)}) %all-to-all-start.4) | async-done | bytes 524320 | tf_op jit(solution)/shard_map/all_to_all | solution.py:167
  70.8 69.0 %while.79 = (s32[]{:T(128)}, f32[2048,128]{0,1:T(8,128)}, f32[2048,128]{1,0:T(8,128)S(1)}, f32[2048,128]{1,0:T(8,128)S(1)}, bf16[2048,1,128]{0,2,1:T(8,128)(2,1)...) while((s32[]{:T(128)}, f32[2048,128]{0,1:T(8,128)}, ...), condition=%wide.region_12.13_spmd, body=%wide.region_5.12_spmd.sunk | while | flops 475268608 | bytes 14478353 | solution.py:139
  71.6 1.9 while.80
  71.8 1.4 fusion.101
  74.7 3.7 %while.81 = (s32[]{:T(128)}, f32[512,128]{1,0:T(8,128)S(1)}, f32[2048,128]{1,0:T(8,128)S(1)}, f32[2048,128]{1,0:T(8,128)S(1)}, s32[]{:T(128)}, /*index=5*/s32[51...) while((s32[]{:T(128)}, f32[512,128]{1,0:T(8,128)S(1)}, ...), condition=%wide.region_11.11_spmd.clone, body=%wide.region_10.10_spmd.clone.sunk | while | flops 338887680 | bytes 5656819 | solution.py:125
  80.5 3.7 %while.80 = (s32[]{:T(128)}, f32[512]{0:T(512)S(1)}, f32[512,128]{1,0:T(8,128)S(1)}, s32[]{:T(128)}, s32[512]{0:T(512)S(1)}, /*index=5*/s32[2048]{0:T(1024)S(1)}...) while((s32[]{:T(128)}, f32[512]{0:T(512)S(1)}, ...), condition=%wide.region_8.8_spmd.clone, body=%wide.region_6.7_spmd.clone.sunk | while | flops 136119296 | bytes 1990855 | solution.py:82
  85.5 7.4 %while.81 = (s32[]{:T(128)}, f32[512,128]{1,0:T(8,128)S(1)}, f32[2048,128]{1,0:T(8,128)S(1)}, f32[2048,128]{1,0:T(8,128)S(1)}, s32[]{:T(128)}, /*index=5*/s32[51...) while((s32[]{:T(128)}, f32[512,128]{1,0:T(8,128)S(1)}, ...), condition=%wide.region_11.11_spmd.clone, body=%wide.region_10.10_spmd.clone.sunk | while | flops 338887680 | bytes 5656819 | solution.py:125
  95.0 5.6 %while.80 = (s32[]{:T(128)}, f32[512]{0:T(512)S(1)}, f32[512,128]{1,0:T(8,128)S(1)}, s32[]{:T(128)}, s32[512]{0:T(512)S(1)}, /*index=5*/s32[2048]{0:T(1024)S(1)}...) while((s32[]{:T(128)}, f32[512]{0:T(512)S(1)}, ...), condition=%wide.region_8.8_spmd.clone, body=%wide.region_6.7_spmd.clone.sunk | while | flops 136119296 | bytes 1990855 | solution.py:82
  95.1 1.4 fusion.101
  101.8 11.1 %while.81 = (s32[]{:T(128)}, f32[512,128]{1,0:T(8,128)S(1)}, f32[2048,128]{1,0:T(8,128)S(1)}, f32[2048,128]{1,0:T(8,128)S(1)}, s32[]{:T(128)}, /*index=5*/s32[51...) while((s32[]{:T(128)}, f32[512,128]{1,0:T(8,128)S(1)}, ...), condition=%wide.region_11.11_spmd.clone, body=%wide.region_10.10_spmd.clone.sunk | while | flops 338887680 | bytes 5656819 | solution.py:125
  115.0 7.5 %while.80 = (s32[]{:T(128)}, f32[512]{0:T(512)S(1)}, f32[512,128]{1,0:T(8,128)S(1)}, s32[]{:T(128)}, s32[512]{0:T(512)S(1)}, /*index=5*/s32[2048]{0:T(1024)S(1)}...) while((s32[]{:T(128)}, f32[512]{0:T(512)S(1)}, ...), condition=%wide.region_8.8_spmd.clone, body=%wide.region_6.7_spmd.clone.sunk | while | flops 136119296 | bytes 1990855 | solution.py:82
  115.2 1.4 fusion.101
  123.7 14.8 %while.81 = (s32[]{:T(128)}, f32[512,128]{1,0:T(8,128)S(1)}, f32[2048,128]{1,0:T(8,128)S(1)}, f32[2048,128]{1,0:T(8,128)S(1)}, s32[]{:T(128)}, /*index=5*/s32[51...) while((s32[]{:T(128)}, f32[512,128]{1,0:T(8,128)S(1)}, ...), condition=%wide.region_11.11_spmd.clone, body=%wide.region_10.10_spmd.clone.sunk | while | flops 338887680 | bytes 5656819 | solution.py:125
  141.2 4.1 %fusion.60 = (f32[2048,1,64]{0,2,1:T(8,128)S(1)}, f32[2048,1,64]{0,2,1:T(8,128)S(1)}, f32[2048,1,64]{0,2,1:T(8,128)S(1)}, f32[2048,1,64]{0,2,1:T(8,128)S(1)}) fusion(f32[2048,1,128]{0,2,1:T(8,128)} %bitcast.159, f32[64]{0:T(128)S(1)} %negate_power_fusion, f32[2048]{0:T(1024)S(1)} %convert_multiply_fusion.1, f32[2048,1,128]{0,2,1:T(8,128)} %bitcast.158), kind=kLoop, calls=%fused_computation.89 | loop fusion | flops 1966080 | bytes 4202752 | tf_op jit(solution)/shard_map/transpose(jvp())/add_any | solution.py:34
  148.6 2.0 reduce.14
  151.8 3.6 %all-to-all-start.5 = ((bf16[16,2,8192]{2,1,0:T(2,128)(2,1)}), bf16[16,2,8192]{2,1,0:T(2,128)(2,1)S(1)}, u32[]{:S(2)}, u32[]{:S(2)}) async-start(bf16[16,2,8192]{2,1,0:T(2,128)(2,1)} %reshape.579), calls=%async_computation.5 | async-start | bytes 1048576 | tf_op jit(solution)/shard_map/all_to_all | solution.py:186
  157.6 6.8 %all-to-all-done.5 = bf16[16,2,8192]{2,1,0:T(2,128)(2,1)S(1)} async-done(((bf16[16,2,8192]{2,1,0:T(2,128)(2,1)}), bf16[16,2,8192]{2,1,0:T(2,128)(2,1)S(1)}, u32[]{:S(2)}, u32[]{:S(2)}) %all-to-all-start.5) | async-done | bytes 524320 | tf_op jit(solution)/shard_map/all_to_all | solution.py:186
  164.3 3.6 %all-to-all-start.6 = ((bf16[16,2,8192]{2,1,0:T(2,128)(2,1)}), bf16[16,2,8192]{2,1,0:T(2,128)(2,1)S(1)}, u32[]{:S(2)}, u32[]{:S(2)}) async-start(bf16[16,2,8192]{2,1,0:T(2,128)(2,1)} %reshape.581), calls=%async_computation.6 | async-start | bytes 1048576 | tf_op jit(solution)/shard_map/all_to_all | solution.py:189
  169.9 6.9 %all-to-all-done.6 = bf16[16,2,8192]{2,1,0:T(2,128)(2,1)S(1)} async-done(((bf16[16,2,8192]{2,1,0:T(2,128)(2,1)}), bf16[16,2,8192]{2,1,0:T(2,128)(2,1)S(1)}, u32[]{:S(2)}, u32[]{:S(2)}) %all-to-all-start.6) | async-done | bytes 524320 | tf_op jit(solution)/shard_map/all_to_all | solution.py:189
  176.9 3.6 %all-to-all-start.7 = ((bf16[16,2,8192]{2,1,0:T(2,128)(2,1)}), bf16[16,2,8192]{2,1,0:T(2,128)(2,1)S(1)}, u32[]{:S(2)}, u32[]{:S(2)}) async-start(bf16[16,2,8192]{2,1,0:T(2,128)(2,1)} %reshape.583), calls=%async_computation.7 | async-start | bytes 1048576 | tf_op jit(solution)/shard_map/all_to_all | solution.py:192
  180.5 117.0 %all-reduce.4 = (f32[128]{0:T(128)}, f32[128]{0:T(128)}) all-reduce(f32[128]{0:T(128)S(1)} %get-tuple-element.430, f32[128]{0:T(128)S(1)} %get-tuple-element.428), channel_id=1, replica_groups=mesh['dp'=32,'seq'=16] {'dp','seq'}, use_global_device_ids=true, to_apply=%region_18.19 | all-reduce | flops 256 | bytes 2048 | tf_op jit(solution)/shard_map/psum | solution.py:201
  (254 shorter events, 93.2 us)
Async XLA Ops:
  0.6 0.7 copy-start.15
  0.6 10.0 %copy-start.10 = (bf16[1,128,16,128]{3,2,1,0:T(8,128)(2,1)S(1)}, bf16[1,128,16,128]{3,2,1,0:T(8,128)(2,1)}, u32[]{:S(2)}) copy-start(bf16[1,128,16,128]{3,2,1,0:T(8,128)(2,1)} %param.13) | copy-start | bytes 1572868
  1.9 13.9 %all-to-all-start.1 = ((s32[16,1,128]{2,1,0:T(1,128)}), s32[16,1,128]{2,1,0:T(1,128)S(1)}, u32[]{:S(2)}, u32[]{:S(2)}) async-start(s32[16,1,128]{2,1,0:T(1,128)} %stack.4), calls=%async_computation.1 | async-start | bytes 16384 | tf_op jit(solution)/shard_map/all_to_all | solution.py:145
  10.7 1.0 copy-start.12
  11.6 1.0 copy-start.11
  15.8 13.4 %all-to-all-start = ((bf16[128,16,128]{2,0,1:T(8,128)(2,1)}), bf16[128,16,128]{2,0,1:T(8,128)(2,1)S(1)}, u32[]{:S(2)}, u32[]{:S(2)}) async-start(bf16[128,16,128]{2,0,1:T(8,128)(2,1)} %bitcast.131), calls=%async_computation | async-start | bytes 1048576 | tf_op jit(solution)/shard_map/all_to_all | solution.py:166
  30.1 12.6 %all-to-all-start.2 = ((bf16[128,16,128]{0,2,1:T(8,128)(2,1)}), bf16[128,16,128]{0,2,1:T(8,128)(2,1)S(1)}, u32[]{:S(2)}, u32[]{:S(2)}) async-start(bf16[128,16,128]{0,2,1:T(8,128)(2,1)} %bitcast.13), calls=%async_computation.2 | async-start | bytes 1048576 | tf_op jit(solution)/shard_map/all_to_all | solution.py:168
  35.2 1.6 copy-start.14
  36.8 1.3 copy-start
  42.8 4.7 %copy-start.2 = (bf16[128,16,128]{0,2,1:T(8,128)(2,1)}, bf16[128,16,128]{0,2,1:T(8,128)(2,1)S(1)}, u32[]{:S(2)}) copy-start(bf16[128,16,128]{0,2,1:T(8,128)(2,1)S(1)} %all-to-all-done.2) | copy-start | bytes 1572868
  43.7 12.5 %all-to-all-start.3 = ((bf16[128,16,128]{2,0,1:T(8,128)(2,1)}), bf16[128,16,128]{2,0,1:T(8,128)(2,1)S(1)}, u32[]{:S(2)}, u32[]{:S(2)}) async-start(bf16[128,16,128]{2,0,1:T(8,128)(2,1)} %bitcast.21), calls=%async_computation.3 | async-start | bytes 1048576 | tf_op jit(solution)/shard_map/all_to_all | solution.py:169
  47.4 0.7 copy-start.13
  48.1 12.4 %copy-start.4 = (f32[2048,1,128]{0,2,1:T(8,128)S(1)}, f32[2048,1,128]{0,2,1:T(8,128)}, u32[]{:S(2)}) copy-start(f32[2048,1,128]{0,2,1:T(8,128)} %multiply_multiply_fusion) | copy-start | bytes 3145732
  49.2 11.3 %copy-start.5 = (f32[2048,1,128]{0,2,1:T(8,128)S(1)}, f32[2048,1,128]{0,2,1:T(8,128)}, u32[]{:S(2)}) copy-start(f32[2048,1,128]{0,2,1:T(8,128)} %fusion.33) | copy-start | bytes 3145732
  56.3 13.2 %all-to-all-start.4 = ((bf16[128,16,128]{2,0,1:T(8,128)(2,1)}), bf16[128,16,128]{2,0,1:T(8,128)(2,1)}, u32[]{:S(2)}, u32[]{:S(2)}) async-start(bf16[128,16,128]{2,0,1:T(8,128)(2,1)} %bitcast.130), calls=%async_computation.4 | async-start | bytes 1048576 | tf_op jit(solution)/shard_map/all_to_all | solution.py:167
  63.7 1.0 copy-start.8
  63.7 1.0 copy-start.9
  70.8 0.8 copy-start.6
  78.6 1.1 copy-start.7
  79.7 0.8 copy-start.6
  93.0 1.1 copy-start.7
  94.2 0.8 copy-start.6
  113.1 1.1 copy-start.7
  114.2 0.8 copy-start.6
  138.7 1.1 copy-start.7
  141.2 4.1 %copy-start.3 = (bf16[128,16,128]{0,2,1:T(8,128)(2,1)S(1)}, bf16[128,16,128]{0,2,1:T(8,128)(2,1)}, u32[]{:S(2)}) copy-start(bf16[128,16,128]{0,2,1:T(8,128)(2,1)} %copy-done.2) | copy-start | bytes 1572868
  145.2 1.2 copy-start.1
  151.8 12.5 %all-to-all-start.5 = ((bf16[16,2,8192]{2,1,0:T(2,128)(2,1)}), bf16[16,2,8192]{2,1,0:T(2,128)(2,1)S(1)}, u32[]{:S(2)}, u32[]{:S(2)}) async-start(bf16[16,2,8192]{2,1,0:T(2,128)(2,1)} %reshape.579), calls=%async_computation.5 | async-start | bytes 1048576 | tf_op jit(solution)/shard_map/all_to_all | solution.py:186
  164.3 12.5 %all-to-all-start.6 = ((bf16[16,2,8192]{2,1,0:T(2,128)(2,1)}), bf16[16,2,8192]{2,1,0:T(2,128)(2,1)S(1)}, u32[]{:S(2)}, u32[]{:S(2)}) async-start(bf16[16,2,8192]{2,1,0:T(2,128)(2,1)} %reshape.581), calls=%async_computation.6 | async-start | bytes 1048576 | tf_op jit(solution)/shard_map/all_to_all | solution.py:189
  176.9 124.0 %all-to-all-start.7 = ((bf16[16,2,8192]{2,1,0:T(2,128)(2,1)}), bf16[16,2,8192]{2,1,0:T(2,128)(2,1)S(1)}, u32[]{:S(2)}, u32[]{:S(2)}) async-start(bf16[16,2,8192]{2,1,0:T(2,128)(2,1)} %reshape.583), calls=%async_computation.7 | async-start | bytes 1048576 | tf_op jit(solution)/shard_map/all_to_all | solution.py:192
